TPU v7x, 256 devices: a whole 4x4x8 slice. The times are simulated.
256 devices in a mesh: gx: 8 (over y, x_lo), gy: 2 (over x_hi), vert: 16 (over z, core).
Axes of the slice: x: 4 (x_hi: 2, x_lo: 2; x = x_hi * 2 + x_lo), y: 4, z: 8, core: 2. Of those that a mesh axis runs over, the one named last changes fastest.
Arguments:
- state: float32 [8000, 3, 4, 1024], P('vert', None, 'gy', 'gx'), as said below
- tangent: float32 [8000, 3, 4, 1024], P('vert', None, 'gy', 'gx')
- orient: int32 [8000, 2], P('vert'), may hold values from 0 to 1, as said below
- walls: int32 [2, 1024], P(None, 'gx'), may hold values from 0 to 1
Outputs:
- product: float32 [8000, 3, 4, 1024], P('vert', None, 'gy', 'gx')
Inputs may be any that keep to these rules, and one draw needn't show every extreme that they name: In every aligned group of four slots 4k to 4k+3 there are two bits p, r with orient[4k + 2b + e] = (e XOR p, b XOR r) for b, e in 0, 1. The state's values at the four points q of every cell are positive.
All inputs are finite; a program needn't handle non-finite values.
Results may differ from a plain program's by a relative error of at most 0.0003.
Values sent between devices are 32-bit elements; how exact they have to be, the bound alone decides.
A program may use at most 64 MiB of HBM per device.

v0:
```python
import math
import jax
import jax.numpy as jnp
from jax import lax
from jax.sharding import PartitionSpec as P

NVX = 20
GAUSS = 0.5773502691896258
XI_SIGNS = (-1.0, -1.0, 1.0, 1.0)
ETA_SIGNS = (-1.0, 1.0, -1.0, 1.0)
MIRRORED_DUOS = ((0, 0), (1, 1), (2, 2), (0, 1), (0, 2), (1, 2))
COLLIDE = 2.0
LOG_TWO_PI = math.log(2.0 * math.pi)


def padded(block, sides, width, periodic):
    for axis, dim in sides:
        count = lax.axis_size(axis)
        forward = [(i, i + 1) for i in range(count - 1)]
        if periodic:
            forward.append((count - 1, 0))
        backward = [(target, source) for source, target in forward]
        low = lax.ppermute(
            lax.slice_in_dim(block, block.shape[dim] - width, None, axis=dim), axis, forward
        )
        high = lax.ppermute(lax.slice_in_dim(block, 0, width, axis=dim), axis, backward)
        block = jnp.concatenate([low, block, high], axis=dim)
    return block


def velocities(slot_index, orient, half_grid):
    spacing = 5.0 / half_grid
    mag_x = (slot_index // (4 * half_grid) % half_grid).astype(jnp.float32) + 0.5
    mag_y = (slot_index // 4 % half_grid).astype(jnp.float32) + 0.5
    level_z = (slot_index // (4 * half_grid * half_grid)).astype(jnp.float32) - (half_grid - 0.5)
    sign_x = (2 * orient[:, 0] - 1).astype(jnp.float32)
    sign_y = (2 * orient[:, 1] - 1).astype(jnp.float32)
    return (sign_x * mag_x * spacing, sign_y * mag_y * spacing, level_z * spacing)


def moment_table(vel_x, vel_y, molecular_grid_extent, weight):
    return (
        jnp.stack(
            [
                jnp.ones_like(vel_x),
                vel_x,
                vel_y,
                molecular_grid_extent,
                vel_x * vel_x,
                vel_y * vel_y,
                molecular_grid_extent * molecular_grid_extent,
                vel_x * vel_y,
                vel_x * molecular_grid_extent,
                vel_y * molecular_grid_extent,
            ]
        )
        * weight
    )


def gauss_points(coef):
    center, grad_x, grad_y = (coef[:, 0], coef[:, 1], coef[:, 2])
    return jnp.stack(
        [center + XI_SIGNS[q] * GAUSS * grad_x + ETA_SIGNS[q] * GAUSS * grad_y for q in range(4)],
        axis=1,
    )


def project_points(values):
    total = values[:, 0] + values[:, 1] + values[:, 2] + values[:, 3]
    along_x = values[:, 2] + values[:, 3] - (values[:, 0] + values[:, 1])
    along_y = values[:, 1] + values[:, 3] - (values[:, 0] + values[:, 2])
    return jnp.stack([0.25 * total, 0.75 * GAUSS * along_x, 0.75 * GAUSS * along_y], axis=1)


def partner(values):
    dims_in = values.shape
    grouped = values.reshape((dims_in[0] // 4, 2, 2) + dims_in[1:])
    return grouped[:, ::-1].reshape(dims_in)


def full_matrix(entries):
    rows = [[None, None, None], [None, None, None], [None, None, None]]
    for duo_ordinal, (leading_multiplier, trailing_multiplier) in enumerate(MIRRORED_DUOS):
        rows[leading_multiplier][trailing_multiplier] = entries[duo_ordinal]
        rows[trailing_multiplier][leading_multiplier] = entries[duo_ordinal]
    return rows


def gauss_params(moments):
    density = moments[0]
    average_offset = [moments[1 + leading_multiplier] / density for leading_multiplier in range(3)]
    second = [moments[4 + duo_ordinal] for duo_ordinal in range(6)]
    covariance_array = [
        second[duo_ordinal] / density
        - average_offset[leading_multiplier] * average_offset[trailing_multiplier]
        for duo_ordinal, (leading_multiplier, trailing_multiplier) in enumerate(MIRRORED_DUOS)
    ]
    thermal_state = (covariance_array[0] + covariance_array[1] + covariance_array[2]) / 3.0
    pressure_dyad = [
        (1.5 * thermal_state if leading_multiplier == trailing_multiplier else 0.0)
        - 0.5 * covariance_array[duo_ordinal]
        for duo_ordinal, (leading_multiplier, trailing_multiplier) in enumerate(MIRRORED_DUOS)
    ]
    tens_full = full_matrix(pressure_dyad)
    cofactor = [
        tens_full[1][1] * tens_full[2][2] - tens_full[1][2] * tens_full[1][2],
        tens_full[0][0] * tens_full[2][2] - tens_full[0][2] * tens_full[0][2],
        tens_full[0][0] * tens_full[1][1] - tens_full[0][1] * tens_full[0][1],
        tens_full[0][2] * tens_full[1][2] - tens_full[0][1] * tens_full[2][2],
        tens_full[0][1] * tens_full[1][2] - tens_full[0][2] * tens_full[1][1],
        tens_full[0][1] * tens_full[0][2] - tens_full[0][0] * tens_full[1][2],
    ]
    determinant = (
        tens_full[0][0] * cofactor[0]
        + tens_full[0][1] * cofactor[3]
        + tens_full[0][2] * cofactor[4]
    )
    inverse = [entry / determinant for entry in cofactor]
    log_pre = jnp.log(density) - 1.5 * LOG_TWO_PI - 0.5 * jnp.log(determinant)
    delta_density = moments[10]
    drift_delta = [
        (moments[11 + leading_multiplier] - average_offset[leading_multiplier] * delta_density)
        / density
        for leading_multiplier in range(3)
    ]
    dtheta = [
        moments[14 + duo_ordinal] / density
        - second[duo_ordinal] * delta_density / (density * density)
        - (
            drift_delta[leading_multiplier] * average_offset[trailing_multiplier]
            + average_offset[leading_multiplier] * drift_delta[trailing_multiplier]
        )
        for duo_ordinal, (leading_multiplier, trailing_multiplier) in enumerate(MIRRORED_DUOS)
    ]
    temp_delta = (dtheta[0] + dtheta[1] + dtheta[2]) / 3.0
    tens_delta = [
        (1.5 * temp_delta if leading_multiplier == trailing_multiplier else 0.0)
        - 0.5 * dtheta[duo_ordinal]
        for duo_ordinal, (leading_multiplier, trailing_multiplier) in enumerate(MIRRORED_DUOS)
    ]
    inv_full = full_matrix(inverse)
    delta_full = full_matrix(tens_delta)
    trace_term = sum(
        [
            inv_full[leading_multiplier][trailing_multiplier]
            * delta_full[trailing_multiplier][leading_multiplier]
            for leading_multiplier in range(3)
            for trailing_multiplier in range(3)
        ]
    )
    shift_term = delta_density / density - 0.5 * trace_term
    weight_vec = [
        inv_full[leading_multiplier][0] * drift_delta[0]
        + inv_full[leading_multiplier][1] * drift_delta[1]
        + inv_full[leading_multiplier][2] * drift_delta[2]
        for leading_multiplier in range(3)
    ]
    inner_prod = [
        [
            inv_full[leading_multiplier][0] * delta_full[0][c]
            + inv_full[leading_multiplier][1] * delta_full[1][c]
            + inv_full[leading_multiplier][2] * delta_full[2][c]
            for c in range(3)
        ]
        for leading_multiplier in range(3)
    ]
    curve_sym = [
        inner_prod[leading_multiplier][0] * inv_full[0][trailing_multiplier]
        + inner_prod[leading_multiplier][1] * inv_full[1][trailing_multiplier]
        + inner_prod[leading_multiplier][2] * inv_full[2][trailing_multiplier]
        for leading_multiplier, trailing_multiplier in MIRRORED_DUOS
    ]
    return jnp.stack(average_offset + inverse + [log_pre, shift_term] + weight_vec + curve_sym)


def quadratic(entries, rel_x, rel_y, rel_z):
    return (
        entries[0] * rel_x * rel_x
        + entries[1] * rel_y * rel_y
        + entries[2] * rel_z * rel_z
        + 2.0
        * (entries[3] * rel_x * rel_y + entries[4] * rel_x * rel_z + entries[5] * rel_y * rel_z)
    )


def gauss_tangent(vel_x, vel_y, molecular_grid_extent, params):
    rel_x = vel_x[:, None] - params[0]
    rel_y = vel_y[:, None] - params[1]
    rel_z = molecular_grid_extent[:, None] - params[2]
    gauss = jnp.exp(params[9] - 0.5 * quadratic(params[3:9], rel_x, rel_y, rel_z))
    return gauss * (
        params[10]
        + rel_x * params[11]
        + rel_y * params[12]
        + rel_z * params[13]
        + 0.5 * quadratic(params[14:20], rel_x, rel_y, rel_z)
    )


def transport(coef, orient, vel_x, vel_y, left_in, right_in, below_in, above_in):
    center, grad_x, grad_y = (coef[:, 0], coef[:, 1], coef[:, 2])
    heads_right = (orient[:, 0] == 1)[:, None, None]
    heads_up = (orient[:, 1] == 1)[:, None, None]
    right_val = jnp.where(heads_right, center + grad_x, right_in[0])
    right_slope = jnp.where(heads_right, grad_y, right_in[1])
    left_val = jnp.where(heads_right, left_in[0], center - grad_x)
    left_slope = jnp.where(heads_right, left_in[1], grad_y)
    top_val = jnp.where(heads_up, center + grad_y, above_in[0])
    top_slope = jnp.where(heads_up, grad_x, above_in[1])
    bottom_val = jnp.where(heads_up, below_in[0], center - grad_y)
    bottom_slope = jnp.where(heads_up, below_in[1], grad_x)
    speed_x = vel_x[:, None, None]
    speed_y = vel_y[:, None, None]
    rate_mean = speed_x * (right_val - left_val) + speed_y * (top_val - bottom_val)
    rate_x = 3.0 * speed_x * (right_val + left_val - 2.0 * center) + speed_y * (
        top_slope - bottom_slope
    )
    rate_y = speed_x * (right_slope - left_slope) + 3.0 * speed_y * (
        top_val + bottom_val - 2.0 * center
    )
    return jnp.stack([rate_mean, rate_x, rate_y], axis=1)


def shards(state, tangent, orient, walls):
    slots_here = state.shape[0]
    cell_rows = state.shape[2]
    cell_cols = state.shape[3]
    half_grid = NVX // 2
    weight = (5.0 / half_grid) ** 3
    point_count = 4 * cell_rows * cell_cols
    slot_index = lax.axis_index("vert") * slots_here + jnp.arange(slots_here, dtype=jnp.int32)
    vel_x, vel_y, molecular_grid_extent = velocities(slot_index, orient, half_grid)
    moment_rows = moment_table(vel_x, vel_y, molecular_grid_extent, weight)
    stacked = jnp.concatenate(
        [
            gauss_points(state).reshape(slots_here, point_count),
            gauss_points(tangent).reshape(slots_here, point_count),
        ],
        axis=1,
    )
    partial_sums = jnp.dot(
        moment_rows, stacked, precision=lax.Precision.HIGHEST, preferred_element_type=jnp.float32
    )
    partial_sums = jnp.concatenate(
        [partial_sums[:, :point_count], partial_sums[:, point_count:]], axis=0
    )
    params = gauss_params(lax.psum(partial_sums, "vert"))
    center, grad_x, grad_y = (tangent[:, 0], tangent[:, 1], tangent[:, 2])
    x_padded = padded(tangent, (("gx", 3),), 1, True)
    western = x_padded[:, :, :, :-2]
    eastern = x_padded[:, :, :, 2:]
    left_in = (western[:, 0] + western[:, 1], western[:, 2])
    right_in = (eastern[:, 0] - eastern[:, 1], eastern[:, 2])
    y_padded = padded(tangent, (("gy", 2),), 1, False)
    southern = y_padded[:, :, :-2]
    northern = y_padded[:, :, 2:]
    below_in = (southern[:, 0] + southern[:, 2], southern[:, 1])
    above_in = (northern[:, 0] - northern[:, 2], northern[:, 1])
    floor_flag = walls[0].astype(jnp.float32)
    roof_flag = walls[1].astype(jnp.float32)
    at_bottom = lax.axis_index("gy") == 0
    at_top = lax.axis_index("gy") == lax.axis_size("gy") - 1
    floor_val = (floor_flag * partner(center - grad_y)[:, 0], floor_flag * partner(grad_x)[:, 0])
    roof_val = (roof_flag * partner(center + grad_y)[:, -1], roof_flag * partner(grad_x)[:, -1])
    below_in = tuple(
        (
            jnp.concatenate(
                [jnp.where(at_bottom, wall_part, field_part[:, 0])[:, None], field_part[:, 1:]],
                axis=1,
            )
            for field_part, wall_part in zip(below_in, floor_val)
        )
    )
    above_in = tuple(
        (
            jnp.concatenate(
                [field_part[:, :-1], jnp.where(at_top, wall_part, field_part[:, -1])[:, None]],
                axis=1,
            )
            for field_part, wall_part in zip(above_in, roof_val)
        )
    )
    advected = transport(tangent, orient, vel_x, vel_y, left_in, right_in, below_in, above_in)
    gauss_delta = gauss_tangent(vel_x, vel_y, molecular_grid_extent, params).reshape(
        slots_here, 4, cell_rows, cell_cols
    )
    return advected + COLLIDE * (tangent - project_points(gauss_delta))


def solution(mesh):
    placed = (
        P("vert", None, "gy", "gx"),
        P("vert", None, "gy", "gx"),
        P("vert", None),
        P(None, "gx"),
    )
    return jax.shard_map(
        shards, mesh=mesh, in_specs=placed, out_specs=P("vert", None, "gy", "gx"), check_vma=False
    )
```

profile of v0, /device:TPU:1, one launch (start us, length us, event | category | flops | bytes accessed | tf_op | source)
XLA Modules:
  0.0 193.0 jit_solution(14825529700817234752)
XLA Ops:
  7.5 2.6 %multiply_add_fusion.9 = (f32[500,1,2,128]{3,2,1,0:T(2,128)S(1)}, f32[500,1,2,128]{3,2,1,0:T(2,128)S(1)}, f32[500,1,2,128]{3,2,1,0:T(2,128)S(1)}, f32[500,1,2,12...) fusion(f32[500,3,2,128]{3,2,1,0:T(2,128)} %param.5), kind=kLoop, calls=%fused_computation.98 | loop fusion | flops 1536000 | bytes 5120000 | tf_op jit(solution)/shard_map/add | solution.py:64
  10.1 1.9 pad_maximum_fusion.1
  12.0 3.9 %reshape.660 = f32[500,1024]{1,0:T(8,128)} reshape(f32[500,4,2,128]{3,2,1,0:T(2,128)} %pad_maximum_fusion.1) | data formatting | bytes 4096000 | tf_op jit(solution)/shard_map/reshape | solution.py:238
  15.8 2.3 %multiply_add_fusion.13 = (f32[500,1,2,128]{3,2,1,0:T(2,128)S(1)}, f32[500,1,2,128]{3,2,1,0:T(2,128)S(1)}, f32[500,1,2,128]{3,2,1,0:T(2,128)S(1)}, f32[500,1,2,128]{3,2,1,0:T(2,128)S(1)}) fusion(f32[500,3,2,128]{3,2,1,0:T(2,128)} %param.4), kind=kLoop, calls=%fused_computation.102 | loop fusion | flops 1280000 | bytes 3584000 | tf_op jit(solution)/shard_map/add | solution.py:64
  18.1 1.9 pad_maximum_fusion
  20.0 3.9 %reshape.659 = f32[500,1024]{1,0:T(8,128)} reshape(f32[500,4,2,128]{3,2,1,0:T(2,128)} %pad_maximum_fusion) | data formatting | bytes 4096000 | tf_op jit(solution)/shard_map/reshape | solution.py:237
  24.0 4.4 %fusion = f32[10,2048]{1,0:T(8,128)S(1)} fusion(f32[500,1024]{1,0:T(8,128)} %reshape.660, f32[500,1024]{1,0:T(8,128)} %reshape.659, f32[10,500]{1,0:T(8,128)S(1)} %stack.11), kind=kOutput, calls=%fused_computation.27 | convolution fusion | flops 123909000 | bytes 4197920 | tf_op jit(solution)/shard_map/dot_general | solution.py:242
  29.1 2.3 %fusion.102 = (f32[500,3,1,128]{3,2,0,1:T(1,128)}, f32[500,3,1,128]{3,2,0,1:T(1,128)}) fusion(f32[500,3,2,128]{3,2,1,0:T(2,128)S(1)} %copy-done), kind=kLoop, calls=%fused_computation.265 | loop fusion | bytes 3072000 | tf_op jit(solution)/shard_map/slice | solution.py:26
  32.7 7.3 %collective-permute-start.3 = (f32[500,3,1,128]{3,2,0,1:T(1,128)}, f32[500,3,1,128]{3,2,0,1:T(1,128)}, u32[]{:S(2)}, u32[]{:S(2)}) collective-permute-start(f32[500,3,1,128]{3,2,0,1:T(1,128)} %get-tuple-element.79), channel_id=1, source_target_pairs={{0,16},{1,17},{2,18},{3,19},{4,20},{5,21},{6,22},{7,23},{8,24},{9,... | collective-permute-start | bytes 2304008 | tf_op jit(solution)/shard_map/ppermute | solution.py:23
  40.0 3.8 %fusion.103 = (f32[500,3,2,1]{3,2,1,0:T(2,128)}, f32[500,3,2,1]{3,2,1,0:T(2,128)}) fusion(f32[500,3,2,128]{3,2,1,0:T(2,128)S(1)} %copy-done), kind=kLoop, calls=%fused_computation.266 | loop fusion | bytes 48000 | tf_op jit(solution)/shard_map/slice | solution.py:26
  43.7 2.5 %copy.33 = f32[500,3,2,1]{0,2,3,1:T(2,128)S(1)} copy(f32[500,3,2,1]{3,2,1,0:T(2,128)} %get-tuple-element.80) | data formatting | bytes 24000
  46.2 4.5 %collective-permute-start = (f32[500,3,2,1]{0,2,3,1:T(2,128)S(1)}, f32[500,3,2,1]{0,2,3,1:T(2,128)S(1)}, u32[]{:S(2)}, u32[]{:S(2)}) collective-permute-start(f32[500,3,2,1]{0,2,3,1:T(2,128)S(1)} %copy.33), channel_id=1, source_target_pairs={{32,0},{64,32},{96,64},{128,96},{160,128},{192,160},{224,192},{0,2... | collective-permute-start | bytes 36008 | tf_op jit(solution)/shard_map/ppermute | solution.py:26
  50.7 2.4 %copy.34 = f32[500,3,2,1]{0,2,3,1:T(2,128)S(1)} copy(f32[500,3,2,1]{3,2,1,0:T(2,128)} %get-tuple-element.81) | data formatting | bytes 24000
  56.4 1.6 collective-permute-done
  60.3 2.0 %copy.20 = f32[500,3,2,1]{3,2,1,0:T(2,128)} copy(f32[500,3,2,1]{0,2,3,1:T(2,128)S(1)} %collective-permute-done.1) | data formatting | bytes 24000 | tf_op jit(solution)/shard_map/ppermute | solution.py:23
  62.3 77.0 %all-reduce.2.cloned.1.call-done = f32[20,1024]{1,0:T(8,128)} async-done(((f32[20,1024]{1,0:T(8,128)}), f32[20,1024]{1,0:T(8,128)}) %all-reduce.2.cloned.1.call-update) | async-done | bytes 81936 | tf_op jit(solution)/shard_map/psum | solution.py:248
  143.8 16.4 %fusion.14 = f32[500,4,2,128]{3,2,1,0:T(2,128)S(1)} fusion(f32[4,2,128]{2,1,0:T(2,128)S(1)} %bitcast.102, f32[4,2,128]{2,1,0:T(2,128)S(1)} %bitcast.105, f32[4,2,128]{2,1,0:T(2,128)S(1)} %bitcast.104, f32[4,2,128]{2,1,0:T(2,128)S(1)} %bitcast.103, f32[4,2,128]{2,1,0:T(2,128)S(1)} %bitcast.106, f32[4,2,128]{2,1,0:T(2,128)S(1)} %bitcast.101, ...), kind=kLoop, calls=%fused_computation.41 | loop fusion | flops 25600000 | bytes 2135920 | tf_op jit(solution)/shard_map/mul | solution.py:192
  161.2 4.0 %fusion.31 = (f32[500,2,128]{2,1,0:T(2,128)S(1)}, f32[500,2,128]{2,1,0:T(2,128)S(1)}, f32[500,2,128]{2,1,0:T(2,128)S(1)}, f32[500,2,128]{2,1,0:T(2,128)S(1)}) fusion(f32[500,3,1,128]{3,2,0,1:T(1,128)} %collective-permute-done.3, f32[500,3,1,128]{3,2,0,1:T(1,128)} %collective-permute-done.2, f32[500,3,2,128]{3,2,1,0:T(2,128)S(1)} %copy-done), kind=kLoop, calls=%fused_computation.66 | loop fusion | flops 1024000 | bytes 5120000 | tf_op jit(solution)/shard_map/squeeze | solution.py:258
  165.8 1.4 fusion.40
  168.2 6.2 %multiply_add_fusion.5 = (f32[500,1,2,128]{3,2,1,0:T(2,128)S(1)}, f32[500,1,2,128]{3,2,1,0:T(2,128)S(1)}, f32[500,1,2,128]{3,2,1,0:T(2,128)S(1)}) fusion(f32[500]{0:T(512)S(1)} %get-tuple-element.122, f32[500]{0:T(512)S(1)} %broadcast_multiply_fusion.3, f32[500,1,2,128]{3,2,1,0:T(2,128)S(1)} %bitcast.76, f32[500,1,2,128]{3,2,1,0:T(2,128)S(1)} %copy-done.3, ...), kind=kLoop, calls=%fused_computation.88 | loop fusion | flops 2304000 | bytes 9221120 | tf_op jit(solution)/shard_map/add | solution.py:215
  174.4 4.7 %fusion.29 = f32[500,1,2,128]{3,2,1,0:T(2,128)S(1)} fusion(f32[500,3,2,128]{3,2,1,0:T(2,128)S(1)} %copy-done, f32[500,3,2,1]{3,2,1,0:T(2,128)S(1)} %copy-done.1, f32[500,3,2,1]{3,2,1,0:T(2,128)S(1)} %copy.18, pred[500]{0:T(512)(128)(4,1)S(1)} %get-tuple-element.6, f32[500]{0:T(512)S(1)} %broadcast_multiply_fusion, f32[500]{0:T(512)S(1)} %broadcast_multiply_fusion.3, ...), kind=kLoop, calls=%fused_computation.62 | loop fusion | flops 1792000 | bytes 8197120 | tf_op jit(solution)/shard_map/add | solution.py:219
  179.1 1.8 broadcast_select_fusion
  180.8 2.8 %multiply_add_fusion.4 = f32[500,1,2,128]{3,2,1,0:T(2,128)S(1)} fusion(f32[500,1,2,128]{3,2,1,0:T(2,128)S(1)} %bitcast.82, f32[500,1,2,128]{3,2,1,0:T(2,128)S(1)} %bitcast.81, f32[500,1,2,128]{3,2,1,0:T(2,128)S(1)} %get-tuple-element.53, f32[500,1,2,128]{3,2,1,0:T(2,128)S(1)} %get-tuple-element.52, pred[500]{0:T(512)(128)(4,1)S(1)} %get-tuple-element.5, ...), kind=kLoop, calls=%fused_computation.87 | loop fusion | flops 1024000 | bytes 3588500 | tf_op jit(solution)/shard_map/add | solution.py:216
  183.7 2.5 %maximum_add_fusion = f32[500,3,2,128]{3,2,1,0:T(2,128)} fusion(f32[500,1,2,128]{3,2,1,0:T(2,128)S(1)} %fusion.29, f32[500,1,2,128]{3,2,1,0:T(2,128)S(1)} %multiply_add_fusion.4, f32[500,1,2,128]{3,2,1,0:T(2,128)S(1)} %get-tuple-element.51, f32[500,3,2,128]{3,2,1,0:T(2,128)S(1)} %copy-done, f32[500,1,2,128]{3,2,1,0:T(2,128)S(1)} %get-tuple-element.64, ...), kind=kLoop, calls=%fused_computation.54 | loop fusion | flops 2688000 | bytes 6144000 | tf_op jit(solution)/shard_map/add | solution.py:288
  (61 shorter events, 15.2 us)
Async XLA Ops:
  6.5 132.8 %all-reduce.2.cloned.1.call-start = ((), (), s32[]{:S(2)}) async-start(), calls=%async_computation | async-start | bytes 196608 | tf_op jit(solution)/shard_map/psum | solution.py:248
  10.0 43.4 %copy-start.2 = (f32[500,1,2,128]{3,2,1,0:T(2,128)}, f32[500,1,2,128]{3,2,1,0:T(2,128)S(1)}, u32[]{:S(2)}) copy-start(f32[500,1,2,128]{3,2,1,0:T(2,128)S(1)} %get-tuple-element.73) | copy-start | bytes 1536004
  10.1 44.3 %copy-start.6 = (f32[500,1,2,128]{3,2,1,0:T(2,128)}, f32[500,1,2,128]{3,2,1,0:T(2,128)S(1)}, u32[]{:S(2)}) copy-start(f32[500,1,2,128]{3,2,1,0:T(2,128)S(1)} %get-tuple-element.74) | copy-start | bytes 1536004
  10.1 45.3 %copy-start.4 = (f32[500,1,2,128]{3,2,1,0:T(2,128)}, f32[500,1,2,128]{3,2,1,0:T(2,128)S(1)}, u32[]{:S(2)}) copy-start(f32[500,1,2,128]{3,2,1,0:T(2,128)S(1)} %get-tuple-element.75) | copy-start | bytes 1536004
  24.0 5.1 %copy-start = (f32[500,3,2,128]{3,2,1,0:T(2,128)S(1)}, f32[500,3,2,128]{3,2,1,0:T(2,128)}, u32[]{:S(2)}) copy-start(f32[500,3,2,128]{3,2,1,0:T(2,128)} %param.5) | copy-start | bytes 4608004
  31.4 129.7 %collective-permute-start.2 = (f32[500,3,1,128]{3,2,0,1:T(1,128)}, f32[500,3,1,128]{3,2,0,1:T(1,128)}, u32[]{:S(2)}, u32[]{:S(2)}) collective-permute-start(f32[500,3,1,128]{3,2,0,1:T(1,128)} %get-tuple-element.78), channel_id=1, source_target_pairs={{16,0},{17,1},{18,2},{19,3},{20,4},{21,5},{22,6},{23,7},{24,8},{25... | collective-permute-start | bytes 2304008 | tf_op jit(solution)/shard_map/ppermute | solution.py:26
  32.7 128.5 %collective-permute-start.3 = (f32[500,3,1,128]{3,2,0,1:T(1,128)}, f32[500,3,1,128]{3,2,0,1:T(1,128)}, u32[]{:S(2)}, u32[]{:S(2)}) collective-permute-start(f32[500,3,1,128]{3,2,0,1:T(1,128)} %get-tuple-element.79), channel_id=1, source_target_pairs={{0,16},{1,17},{2,18},{3,19},{4,20},{5,21},{6,22},{7,23},{8,24},{9,... | collective-permute-start | bytes 2304008 | tf_op jit(solution)/shard_map/ppermute | solution.py:23
  43.7 9.6 %copy-start.11 = (s32[500,2]{0,1:T(2,128)S(1)}, s32[500,2]{0,1:T(2,128)}, u32[]{:S(2)}) copy-start(s32[500,2]{0,1:T(2,128)} %param.6) | copy-start | bytes 12004
  43.7 9.6 %copy-start.12 = (s32[2,128]{1,0:T(2,128)S(1)}, s32[2,128]{1,0:T(2,128)}, u32[]{:S(2)}) copy-start(s32[2,128]{1,0:T(2,128)} %param.7) | copy-start | bytes 3076
  46.2 11.8 %collective-permute-start = (f32[500,3,2,1]{0,2,3,1:T(2,128)S(1)}, f32[500,3,2,1]{0,2,3,1:T(2,128)S(1)}, u32[]{:S(2)}, u32[]{:S(2)}) collective-permute-start(f32[500,3,2,1]{0,2,3,1:T(2,128)S(1)} %copy.33), channel_id=1, source_target_pairs={{32,0},{64,32},{96,64},{128,96},{160,128},{192,160},{224,192},{0,2... | collective-permute-start | bytes 36008 | tf_op jit(solution)/shard_map/ppermute | solution.py:26
  53.2 7.1 %collective-permute-start.1 = (f32[500,3,2,1]{0,2,3,1:T(2,128)S(1)}, f32[500,3,2,1]{0,2,3,1:T(2,128)S(1)}, u32[]{:S(2)}, u32[]{:S(2)}) collective-permute-start(f32[500,3,2,1]{0,2,3,1:T(2,128)S(1)} %copy.34), channel_id=1, source_target_pairs={{0,32},{32,64},{64,96},{96,128},{128,160},{160,192},{192,224},{224... | collective-permute-start | bytes 36008 | tf_op jit(solution)/shard_map/ppermute | solution.py:23
  161.1 4.1 %copy-start.10 = (f32[125,2,2,2,128]{4,3,2,1,0:T(2,128)S(1)}, f32[125,2,2,2,128]{4,3,2,1,0:T(2,128)}, u32[]{:S(2)}) copy-start(f32[125,2,2,2,128]{4,3,2,1,0:T(2,128)} %rev.10) | copy-start | bytes 1536004
  161.1 4.6 %copy-start.8 = (f32[125,2,2,2,128]{4,3,2,1,0:T(2,128)S(1)}, f32[125,2,2,2,128]{4,3,2,1,0:T(2,128)}, u32[]{:S(2)}) copy-start(f32[125,2,2,2,128]{4,3,2,1,0:T(2,128)} %rev.12) | copy-start | bytes 1536004
  161.1 4.6 %copy-start.9 = (f32[125,2,2,2,128]{4,3,2,1,0:T(2,128)S(1)}, f32[125,2,2,2,128]{4,3,2,1,0:T(2,128)}, u32[]{:S(2)}) copy-start(f32[125,2,2,2,128]{4,3,2,1,0:T(2,128)} %rev.11) | copy-start | bytes 1536004
  165.8 2.3 %copy-start.1 = (f32[500,3,2,1]{3,2,1,0:T(2,128)S(1)}, f32[500,3,2,1]{3,2,1,0:T(2,128)}, u32[]{:S(2)}) copy-start(f32[500,3,2,1]{3,2,1,0:T(2,128)} %copy.20) | copy-start | bytes 36004
  165.8 2.3 %copy-start.3 = (f32[500,1,2,128]{3,2,1,0:T(2,128)S(1)}, f32[500,1,2,128]{3,2,1,0:T(2,128)}, u32[]{:S(2)}) copy-start(f32[500,1,2,128]{3,2,1,0:T(2,128)} %copy-done.2) | copy-start | bytes 1536004
  165.8 2.3 %copy-start.5 = (f32[500,1,2,128]{3,2,1,0:T(2,128)S(1)}, f32[500,1,2,128]{3,2,1,0:T(2,128)}, u32[]{:S(2)}) copy-start(f32[500,1,2,128]{3,2,1,0:T(2,128)} %copy-done.4) | copy-start | bytes 1536004
  174.4 4.7 %copy-start.7 = (f32[500,1,2,128]{3,2,1,0:T(2,128)S(1)}, f32[500,1,2,128]{3,2,1,0:T(2,128)}, u32[]{:S(2)}) copy-start(f32[500,1,2,128]{3,2,1,0:T(2,128)} %copy-done.6) | copy-start | bytes 1536004
Sparse Core Ops, SparseCore 0:
  29.2 110.0 all-reduce.1
where the time goes:
time: 194 us; the launch traced here: 193 us
  waiting for transfers between devices  79.8 us (41%)
  other arithmetic  56.9 us (29%)
  local copies, waits for them, and re-layouts  25 us (13%)
  between operations  13.8 us (7%)
  starting transfers between devices  13.2 us (7%)
  matrix products  4.37 us (2%)
    psum x1, waiting for transfers between devices, shards(): params = gauss_params(lax.psum(partial_sums, 'vert'))  77 us
    mul x1, other arithmetic, gauss_tangent(): gauss * (params[10] + rel_x * params[11] + rel_y * params[12] + rel_z * p...  16.4 us
    ppermute x2, starting transfers between devices, padded(): lax.ppermute(lax.slice_in_dim(block, block.shape[dim] - width, None, axis...  7.33 us
    add x1, other arithmetic, transport(): speed_x * (right_val - left_val) + speed_y * (top_val - bottom_val)  6.21 us
    slice x2, local copies, waits for them, and re-layouts, padded(): lax.slice_in_dim(block, 0, width, axis=dim)  6.09 us
    ppermute x2, starting transfers between devices, padded(): lax.ppermute(lax.slice_in_dim(block, 0, width, axis=dim), axis, backward)  5.82 us
    unnamed x28, local copies, waits for them, and re-layouts  4.98 us
    add x2, other arithmetic, gauss_points(): center + XI_SIGNS[q] * GAUSS * grad_x + ETA_SIGNS[q] * GAUSS * grad_y  4.89 us
  transfers between devices with their start and end apart: 5, of which 3 were waited for; matrix products, arithmetic and copies ran while one was open for 20% of the time, Pallas kernels for 0%

commit v1 on v0

--- a/solution.py
+++ b/solution.py
@@ -11,6 +11,11 @@
 MIRRORED_DUOS = ((0, 0), (1, 1), (2, 2), (0, 1), (0, 2), (1, 2))
 COLLIDE = 2.0
 LOG_TWO_PI = math.log(2.0 * math.pi)
+
+
+def summed_here(value, axis):
+    blocks = lax.all_gather(value, axis)
+    return jnp.sum(blocks, axis=0)
 
 
 def padded(block, sides, width, periodic):
@@ -245,7 +250,7 @@
     partial_sums = jnp.concatenate(
         [partial_sums[:, :point_count], partial_sums[:, point_count:]], axis=0
     )
-    params = gauss_params(lax.psum(partial_sums, "vert"))
+    params = gauss_params(summed_here(partial_sums, "vert"))
     center, grad_x, grad_y = (tangent[:, 0], tangent[:, 1], tangent[:, 2])
     x_padded = padded(tangent, (("gx", 3),), 1, True)
     western = x_padded[:, :, :, :-2]

time: 194 us -> 118 us (0.61)
  waiting for transfers between devices: 79.8 us -> 2.79 us
    psum x1 -> x0, waiting for transfers between devices: 77 us -> none  [shards(): params = gauss_params(lax.psum(partial_sums, 'vert'))]
    sub x2, other arithmetic: 2.27 us -> 0.1 us  [gauss_params(): moments[14 + duo_ordinal] / density]
    unnamed x28 -> x34, local copies, waits for them, and re-layouts: 4.98 us -> 5.48 us
  transfers between devices with their start and end apart: 5 -> 5, of which waited for: 3 -> 2; matrix products, arithmetic and copies ran while one was open for 20% -> 36% of each run, Pallas kernels for 0% -> 0%
where the time goes in v1:
time: 118 us; the launch traced here: 116 us
  other arithmetic  56.9 us (48%)
  local copies, waits for them, and re-layouts  25.5 us (22%)
  between operations  13.8 us (12%)
  starting transfers between devices  13.1 us (11%)
  matrix products  4.37 us (4%)
  waiting for transfers between devices  2.79 us (2%)
    mul x1, other arithmetic, gauss_tangent(): gauss * (params[10] + rel_x * params[11] + rel_y * params[12] + rel_z * p...  16.4 us
    ppermute x2, starting transfers between devices, padded(): lax.ppermute(lax.slice_in_dim(block, block.shape[dim] - width, None, axis...  7.34 us
    add x1, other arithmetic, transport(): speed_x * (right_val - left_val) + speed_y * (top_val - bottom_val)  6.84 us
    slice x2, local copies, waits for them, and re-layouts, padded(): lax.slice_in_dim(block, 0, width, axis=dim)  6.07 us
    add x1, other arithmetic, transport(): speed_x * (right_slope - left_slope)  5.84 us
    ppermute x2, starting transfers between devices, padded(): lax.ppermute(lax.slice_in_dim(block, 0, width, axis=dim), axis, backward)  5.78 us
    unnamed x34, local copies, waits for them, and re-layouts  5.48 us
    add x2, other arithmetic, gauss_points(): center + XI_SIGNS[q] * GAUSS * grad_x + ETA_SIGNS[q] * GAUSS * grad_y  4.89 us
  transfers between devices with their start and end apart: 5, of which 2 were waited for; matrix products, arithmetic and copies ran while one was open for 36% of the time, Pallas kernels for 0%

profile of v1, /device:TPU:1, one launch (start us, length us, event | category | flops | bytes accessed | tf_op | source)
XLA Modules:
  0.0 116.5 jit_solution(10327730085306393507)
XLA Ops:
  7.5 2.6 %multiply_add_fusion.9 = (f32[500,1,2,128]{3,2,1,0:T(2,128)S(1)}, f32[500,1,2,128]{3,2,1,0:T(2,128)S(1)}, f32[500,1,2,128]{3,2,1,0:T(2,128)S(1)}, f32[500,1,2,12...) fusion(f32[500,3,2,128]{3,2,1,0:T(2,128)} %param.5), kind=kLoop, calls=%fused_computation.98 | loop fusion | flops 1536000 | bytes 5120000 | tf_op jit(solution)/shard_map/add | solution.py:69
  10.1 1.9 %pad_maximum_fusion.1 = f32[500,4,2,128]{3,2,1,0:T(2,128)} fusion(f32[500,1,2,128]{3,2,1,0:T(2,128)S(1)} %get-tuple-element.71, f32[500,1,2,128]{3,2,1,0:T(2,128)S(1)} %get-tuple-element.72, f32[500,1,2,128]{3,2,1,0:T(2,128)S(1)} %get-tuple-element.70, f32[500,1,2,128]{3,2,1,0:T(2,128)S(1)} %get-tuple-element.69), kind=kLoop, calls=%fused_computation.53 | loop fusion | flops 1536000 | bytes 4096000 | tf_op jit(solution)/shard_map/stack | solution.py:68
  12.0 3.9 %reshape.660 = f32[500,1024]{1,0:T(8,128)} reshape(f32[500,4,2,128]{3,2,1,0:T(2,128)} %pad_maximum_fusion.1) | data formatting | bytes 4096000 | tf_op jit(solution)/shard_map/reshape | solution.py:243
  15.9 2.3 %multiply_add_fusion.13 = (f32[500,1,2,128]{3,2,1,0:T(2,128)S(1)}, f32[500,1,2,128]{3,2,1,0:T(2,128)S(1)}, f32[500,1,2,128]{3,2,1,0:T(2,128)S(1)}, f32[500,1,2,128]{3,2,1,0:T(2,128)S(1)}) fusion(f32[500,3,2,128]{3,2,1,0:T(2,128)} %param.4), kind=kLoop, calls=%fused_computation.102 | loop fusion | flops 1280000 | bytes 3584000 | tf_op jit(solution)/shard_map/add | solution.py:69
  18.2 1.9 %pad_maximum_fusion = f32[500,4,2,128]{3,2,1,0:T(2,128)} fusion(f32[500,1,2,128]{3,2,1,0:T(2,128)S(1)} %get-tuple-element.67, f32[500,1,2,128]{3,2,1,0:T(2,128)S(1)} %get-tuple-element.66, f32[500,1,2,128]{3,2,1,0:T(2,128)S(1)} %get-tuple-element.68, f32[500,1,2,128]{3,2,1,0:T(2,128)S(1)} %get-tuple-element.65), kind=kLoop, calls=%fused_computation.52 | loop fusion | flops 1536000 | bytes 4096000 | tf_op jit(solution)/shard_map/stack | solution.py:68
  20.1 3.9 %reshape.659 = f32[500,1024]{1,0:T(8,128)} reshape(f32[500,4,2,128]{3,2,1,0:T(2,128)} %pad_maximum_fusion) | data formatting | bytes 4096000 | tf_op jit(solution)/shard_map/reshape | solution.py:242
  24.1 4.4 %fusion = f32[10,2048]{1,0:T(8,128)S(1)} fusion(f32[500,1024]{1,0:T(8,128)} %reshape.660, f32[500,1024]{1,0:T(8,128)} %reshape.659, f32[10,500]{1,0:T(8,128)S(1)} %stack.11), kind=kOutput, calls=%fused_computation.27 | convolution fusion | flops 123909000 | bytes 4197920 | tf_op jit(solution)/shard_map/dot_general | solution.py:247
  29.2 2.3 %fusion.102 = (f32[500,3,1,128]{3,2,0,1:T(1,128)}, f32[500,3,1,128]{3,2,0,1:T(1,128)}) fusion(f32[500,3,2,128]{3,2,1,0:T(2,128)S(1)} %copy-done), kind=kLoop, calls=%fused_computation.265 | loop fusion | bytes 3072000 | tf_op jit(solution)/shard_map/slice | solution.py:31
  32.8 7.3 %collective-permute-start.3 = (f32[500,3,1,128]{3,2,0,1:T(1,128)}, f32[500,3,1,128]{3,2,0,1:T(1,128)}, u32[]{:S(2)}, u32[]{:S(2)}) collective-permute-start(f32[500,3,1,128]{3,2,0,1:T(1,128)} %get-tuple-element.79), channel_id=1, source_target_pairs={{0,16},{1,17},{2,18},{3,19},{4,20},{5,21},{6,22},{7,23},{8,24},{9,... | collective-permute-start | bytes 2304008 | tf_op jit(solution)/shard_map/ppermute | solution.py:28
  40.0 3.8 %fusion.103 = (f32[500,3,2,1]{3,2,1,0:T(2,128)}, f32[500,3,2,1]{3,2,1,0:T(2,128)}) fusion(f32[500,3,2,128]{3,2,1,0:T(2,128)S(1)} %copy-done), kind=kLoop, calls=%fused_computation.266 | loop fusion | bytes 48000 | tf_op jit(solution)/shard_map/slice | solution.py:31
  43.8 2.5 %copy.33 = f32[500,3,2,1]{0,2,3,1:T(2,128)S(1)} copy(f32[500,3,2,1]{3,2,1,0:T(2,128)} %get-tuple-element.80) | data formatting | bytes 24000
  46.3 4.5 %collective-permute-start = (f32[500,3,2,1]{0,2,3,1:T(2,128)S(1)}, f32[500,3,2,1]{0,2,3,1:T(2,128)S(1)}, u32[]{:S(2)}, u32[]{:S(2)}) collective-permute-start(f32[500,3,2,1]{0,2,3,1:T(2,128)S(1)} %copy.33), channel_id=1, source_target_pairs={{32,0},{64,32},{96,64},{128,96},{160,128},{192,160},{224,192},{0,2... | collective-permute-start | bytes 36008 | tf_op jit(solution)/shard_map/ppermute | solution.py:31
  50.8 2.5 %copy.34 = f32[500,3,2,1]{0,2,3,1:T(2,128)S(1)} copy(f32[500,3,2,1]{3,2,1,0:T(2,128)} %get-tuple-element.81) | data formatting | bytes 24000
  58.7 1.6 %collective-permute-done.1 = f32[500,3,2,1]{0,2,3,1:T(2,128)S(1)} collective-permute-done((f32[500,3,2,1]{0,2,3,1:T(2,128)S(1)}, f32[500,3,2,1]{0,2,3,1:T(2,128)S(1)}, u32[]{:S(2)}, u32[]{:S(2)}) %collective-permute-start.1) | collective-permute-done | bytes 12032 | tf_op jit(solution)/shard_map/ppermute | solution.py:28
  60.3 2.0 %copy.20 = f32[500,3,2,1]{3,2,1,0:T(2,128)} copy(f32[500,3,2,1]{0,2,3,1:T(2,128)S(1)} %collective-permute-done.1) | data formatting | bytes 24000 | tf_op jit(solution)/shard_map/ppermute | solution.py:28
  62.4 4.0 %fusion.31 = (f32[500,2,128]{2,1,0:T(2,128)S(1)}, f32[500,2,128]{2,1,0:T(2,128)S(1)}, f32[500,2,128]{2,1,0:T(2,128)S(1)}, f32[500,2,128]{2,1,0:T(2,128)S(1)}) fusion(f32[500,3,1,128]{3,2,0,1:T(1,128)} %collective-permute-done.3, f32[500,3,1,128]{3,2,0,1:T(1,128)} %collective-permute-done.2, f32[500,3,2,128]{3,2,1,0:T(2,128)S(1)} %copy-done), kind=kLoop, calls=%fused_computation.66 | loop fusion | flops 1024000 | bytes 5120000 | tf_op jit(solution)/shard_map/squeeze | solution.py:263
  66.4 1.4 %fusion.40 = (f32[500,1,1,128]{3,1,2,0:T(1,128)S(1)}, f32[500,1,1,128]{3,1,2,0:T(1,128)S(1)}, f32[500,1,1,128]{3,1,2,0:T(1,128)S(1)}, f32[500,1,1,128]{3,1,2,0:T...) fusion(pred[]{:T(512)S(6)} %eq.34, f32[500,2,128]{2,1,0:T(2,128)S(1)} %get-tuple-element.58, ...), kind=kLoop, calls=%fused_computation.106 | loop fusion | flops 384000 | bytes 3841026 | tf_op jit(solution)/shard_map/concatenate | solution.py:273
  68.8 1.8 %broadcast_select_fusion = f32[500,1,2,128]{3,1,2,0:T(1,128)S(1)} fusion(f32[500,1,2,128]{3,1,2,0:T(1,128)S(1)} %bitcast.81, pred[500]{0:T(512)(128)(4,1)S(1)} %get-tuple-element.5, f32[500,1,1,128]{3,1,2,0:T(1,128)S(1)} %get-tuple-element.83, f32[500,1,1,128]{3,1,2,0:T(1,128)S(1)} %get-tuple-element.84), kind=kLoop, calls=%fused_computation.57 | loop fusion | flops 256000 | bytes 1536500 | tf_op jit(solution)/shard_map/jit(_where)/select_n | solution.py:215
  71.1 6.8 %multiply_add_fusion.5 = (f32[500,1,2,128]{3,2,1,0:T(2,128)}, f32[500,1,2,128]{3,2,1,0:T(2,128)S(1)}, f32[500,1,2,128]{3,2,1,0:T(2,128)S(1)}) fusion(f32[500]{0:T(512)S(1)} %get-tuple-element.122, f32[500]{0:T(512)S(1)} %broadcast_multiply_fusion.3, f32[500,1,2,128]{3,2,1,0:T(2,128)S(1)} %bitcast.78, f32[500,1,2,128]{3,2,1,0:T(2,128)S(1)} %copy-done.3, ...), kind=kLoop, calls=%fused_computation.88 | loop fusion | flops 2304000 | bytes 9221120 | tf_op jit(solution)/shard_map/add | solution.py:220
  78.0 3.6 %multiply_add_fusion.4 = f32[500,1,2,128]{3,2,1,0:T(2,128)} fusion(f32[500,1,2,128]{3,2,1,0:T(2,128)S(1)} %bitcast.84, f32[500,1,2,128]{3,2,1,0:T(2,128)S(1)} %bitcast.83, f32[500,1,2,128]{3,2,1,0:T(2,128)S(1)} %get-tuple-element.53, f32[500,1,2,128]{3,2,1,0:T(2,128)S(1)} %get-tuple-element.52, pred[500]{0:T(512)(128)(4,1)S(1)} %get-tuple-element.5, ...), kind=kLoop, calls=%fused_computation.87 | loop fusion | flops 1024000 | bytes 3588500 | tf_op jit(solution)/shard_map/add | solution.py:221
  81.6 5.8 %fusion.29 = f32[500,1,2,128]{3,2,1,0:T(2,128)} fusion(f32[500,3,2,128]{3,2,1,0:T(2,128)S(1)} %copy-done, f32[500,3,2,1]{3,2,1,0:T(2,128)S(1)} %copy-done.1, f32[500,3,2,1]{3,2,1,0:T(2,128)S(1)} %copy.18, pred[500]{0:T(512)(128)(4,1)S(1)} %get-tuple-element.6, f32[500]{0:T(512)S(1)} %broadcast_multiply_fusion, f32[500]{0:T(512)S(1)} %broadcast_multiply_fusion.3, ...), kind=kLoop, calls=%fused_computation.62 | loop fusion | flops 1792000 | bytes 8197120 | tf_op jit(solution)/shard_map/add | solution.py:224
  87.4 1.5 %reduce_sum.9 = f32[20,1024]{1,0:T(8,128)S(1)} reduce(f32[16,20,1024]{2,1,0:T(8,128)} %all-gather.4.cloned.1.call-done, f32[]{:T(128)} %constant.94.clone.1), dimensions={0}, to_apply=%region_0.1 | reduce | flops 307200 | bytes 1392644 | tf_op jit(solution)/shard_map/reduce_sum | solution.py:18
  89.4 16.4 %fusion.14 = f32[500,4,2,128]{3,2,1,0:T(2,128)S(1)} fusion(f32[4,2,128]{2,1,0:T(2,128)S(1)} %bitcast.104, f32[4,2,128]{2,1,0:T(2,128)S(1)} %bitcast.107, f32[4,2,128]{2,1,0:T(2,128)S(1)} %bitcast.106, f32[4,2,128]{2,1,0:T(2,128)S(1)} %bitcast.105, f32[4,2,128]{2,1,0:T(2,128)S(1)} %bitcast.108, f32[4,2,128]{2,1,0:T(2,128)S(1)} %bitcast.103, ...), kind=kLoop, calls=%fused_computation.41 | loop fusion | flops 25600000 | bytes 2135920 | tf_op jit(solution)/shard_map/mul | solution.py:197
  107.2 2.4 %maximum_add_fusion = f32[500,3,2,128]{3,2,1,0:T(2,128)} fusion(f32[500,1,2,128]{3,2,1,0:T(2,128)S(1)} %copy-done.9, f32[500,1,2,128]{3,2,1,0:T(2,128)S(1)} %copy-done.10, f32[500,1,2,128]{3,2,1,0:T(2,128)S(1)} %copy-done.8, f32[500,3,2,128]{3,2,1,0:T(2,128)S(1)} %copy-done, f32[500,1,2,128]{3,2,1,0:T(2,128)S(1)} %get-tuple-element.64, ...), kind=kLoop, calls=%fused_computation.54 | loop fusion | flops 2688000 | bytes 6144000 | tf_op jit(solution)/shard_map/add | solution.py:293
  (68 shorter events, 11.6 us)
Async XLA Ops:
  6.5 80.9 %all-gather.4.cloned.1.call-start = ((), (), s32[]{:S(2)}) async-start(), calls=%async_computation | async-start | bytes 1671168 | tf_op jit(solution)/shard_map/all_gather | solution.py:17
  10.0 43.4 %copy-start.2 = (f32[500,1,2,128]{3,2,1,0:T(2,128)}, f32[500,1,2,128]{3,2,1,0:T(2,128)S(1)}, u32[]{:S(2)}) copy-start(f32[500,1,2,128]{3,2,1,0:T(2,128)S(1)} %get-tuple-element.73) | copy-start | bytes 1536004
  10.1 44.4 %copy-start.6 = (f32[500,1,2,128]{3,2,1,0:T(2,128)}, f32[500,1,2,128]{3,2,1,0:T(2,128)S(1)}, u32[]{:S(2)}) copy-start(f32[500,1,2,128]{3,2,1,0:T(2,128)S(1)} %get-tuple-element.74) | copy-start | bytes 1536004
  10.1 45.4 %copy-start.4 = (f32[500,1,2,128]{3,2,1,0:T(2,128)}, f32[500,1,2,128]{3,2,1,0:T(2,128)S(1)}, u32[]{:S(2)}) copy-start(f32[500,1,2,128]{3,2,1,0:T(2,128)S(1)} %get-tuple-element.75) | copy-start | bytes 1536004
  24.1 5.1 %copy-start = (f32[500,3,2,128]{3,2,1,0:T(2,128)S(1)}, f32[500,3,2,128]{3,2,1,0:T(2,128)}, u32[]{:S(2)}) copy-start(f32[500,3,2,128]{3,2,1,0:T(2,128)} %param.5) | copy-start | bytes 4608004
  31.5 30.9 %collective-permute-start.2 = (f32[500,3,1,128]{3,2,0,1:T(1,128)}, f32[500,3,1,128]{3,2,0,1:T(1,128)}, u32[]{:S(2)}, u32[]{:S(2)}) collective-permute-start(f32[500,3,1,128]{3,2,0,1:T(1,128)} %get-tuple-element.78), channel_id=1, source_target_pairs={{16,0},{17,1},{18,2},{19,3},{20,4},{21,5},{22,6},{23,7},{24,8},{25... | collective-permute-start | bytes 2304008 | tf_op jit(solution)/shard_map/ppermute | solution.py:31
  32.8 29.6 %collective-permute-start.3 = (f32[500,3,1,128]{3,2,0,1:T(1,128)}, f32[500,3,1,128]{3,2,0,1:T(1,128)}, u32[]{:S(2)}, u32[]{:S(2)}) collective-permute-start(f32[500,3,1,128]{3,2,0,1:T(1,128)} %get-tuple-element.79), channel_id=1, source_target_pairs={{0,16},{1,17},{2,18},{3,19},{4,20},{5,21},{6,22},{7,23},{8,24},{9,... | collective-permute-start | bytes 2304008 | tf_op jit(solution)/shard_map/ppermute | solution.py:28
  43.8 9.6 %copy-start.14 = (s32[500,2]{0,1:T(2,128)S(1)}, s32[500,2]{0,1:T(2,128)}, u32[]{:S(2)}) copy-start(s32[500,2]{0,1:T(2,128)} %param.6) | copy-start | bytes 12004
  43.8 9.6 %copy-start.15 = (s32[2,128]{1,0:T(2,128)S(1)}, s32[2,128]{1,0:T(2,128)}, u32[]{:S(2)}) copy-start(s32[2,128]{1,0:T(2,128)} %param.7) | copy-start | bytes 3076
  46.3 11.3 %collective-permute-start = (f32[500,3,2,1]{0,2,3,1:T(2,128)S(1)}, f32[500,3,2,1]{0,2,3,1:T(2,128)S(1)}, u32[]{:S(2)}, u32[]{:S(2)}) collective-permute-start(f32[500,3,2,1]{0,2,3,1:T(2,128)S(1)} %copy.33), channel_id=1, source_target_pairs={{32,0},{64,32},{96,64},{128,96},{160,128},{192,160},{224,192},{0,2... | collective-permute-start | bytes 36008 | tf_op jit(solution)/shard_map/ppermute | solution.py:31
  53.3 7.1 %collective-permute-start.1 = (f32[500,3,2,1]{0,2,3,1:T(2,128)S(1)}, f32[500,3,2,1]{0,2,3,1:T(2,128)S(1)}, u32[]{:S(2)}, u32[]{:S(2)}) collective-permute-start(f32[500,3,2,1]{0,2,3,1:T(2,128)S(1)} %copy.34), channel_id=1, source_target_pairs={{0,32},{32,64},{64,96},{96,128},{128,160},{160,192},{192,224},{224... | collective-permute-start | bytes 36008 | tf_op jit(solution)/shard_map/ppermute | solution.py:28
  62.4 4.0 %copy-start.11 = (f32[125,2,2,2,128]{4,3,2,1,0:T(2,128)S(1)}, f32[125,2,2,2,128]{4,3,2,1,0:T(2,128)}, u32[]{:S(2)}) copy-start(f32[125,2,2,2,128]{4,3,2,1,0:T(2,128)} %rev.12) | copy-start | bytes 1536004
  62.4 4.0 %copy-start.12 = (f32[125,2,2,2,128]{4,3,2,1,0:T(2,128)S(1)}, f32[125,2,2,2,128]{4,3,2,1,0:T(2,128)}, u32[]{:S(2)}) copy-start(f32[125,2,2,2,128]{4,3,2,1,0:T(2,128)} %rev.11) | copy-start | bytes 1536004
  66.4 2.4 %copy-start.7 = (f32[500,1,2,128]{3,2,1,0:T(2,128)S(1)}, f32[500,1,2,128]{3,2,1,0:T(2,128)}, u32[]{:S(2)}) copy-start(f32[500,1,2,128]{3,2,1,0:T(2,128)} %copy-done.6) | copy-start | bytes 1536004
  67.8 2.7 %copy-start.13 = (f32[125,2,2,2,128]{4,3,2,1,0:T(2,128)S(1)}, f32[125,2,2,2,128]{4,3,2,1,0:T(2,128)}, u32[]{:S(2)}) copy-start(f32[125,2,2,2,128]{4,3,2,1,0:T(2,128)} %rev.10) | copy-start | bytes 1536004
  67.8 3.3 %copy-start.1 = (f32[500,3,2,1]{3,2,1,0:T(2,128)S(1)}, f32[500,3,2,1]{3,2,1,0:T(2,128)}, u32[]{:S(2)}) copy-start(f32[500,3,2,1]{3,2,1,0:T(2,128)} %copy.20) | copy-start | bytes 36004
  67.8 3.3 %copy-start.3 = (f32[500,1,2,128]{3,2,1,0:T(2,128)S(1)}, f32[500,1,2,128]{3,2,1,0:T(2,128)}, u32[]{:S(2)}) copy-start(f32[500,1,2,128]{3,2,1,0:T(2,128)} %copy-done.2) | copy-start | bytes 1536004
  67.8 3.3 %copy-start.5 = (f32[500,1,2,128]{3,2,1,0:T(2,128)S(1)}, f32[500,1,2,128]{3,2,1,0:T(2,128)}, u32[]{:S(2)}) copy-start(f32[500,1,2,128]{3,2,1,0:T(2,128)} %copy-done.4) | copy-start | bytes 1536004
  105.8 1.0 copy-start.8
  105.9 1.2 %copy-start.9 = (f32[500,1,2,128]{3,2,1,0:T(2,128)S(1)}, f32[500,1,2,128]{3,2,1,0:T(2,128)}, u32[]{:S(2)}) copy-start(f32[500,1,2,128]{3,2,1,0:T(2,128)} %fusion.29) | copy-start | bytes 1536004
  105.9 1.3 %copy-start.10 = (f32[500,1,2,128]{3,2,1,0:T(2,128)S(1)}, f32[500,1,2,128]{3,2,1,0:T(2,128)}, u32[]{:S(2)}) copy-start(f32[500,1,2,128]{3,2,1,0:T(2,128)} %multiply_add_fusion.4) | copy-start | bytes 1536004
Sparse Core Ops, SparseCore 0:
  29.3 43.0 all-gather.3
